TPU v7x, 32 devices: a whole 2x2x4 slice. The times are simulated.
32 devices in a mesh: tok: 8 (over z, x), col: 4 (over y, core).
Axes of the slice: x: 2, y: 2, z: 4, core: 2. Of those that a mesh axis runs over, the one named last changes fastest.
Arguments:
- tokens: bfloat16 [2560, 4096], P('tok', 'col'), may hold values from -16 to 16
- w_query: bfloat16 [4096, 2048], P(None, 'col'), may hold values from -0.09375 to 0.09375
- w_key: bfloat16 [4096, 512], P(None, 'col'), may hold values from -0.09375 to 0.09375
- w_value: bfloat16 [4096, 512], P(None, 'col'), may hold values from -0.09375 to 0.09375
- w_out: bfloat16 [2048, 4096], P('col'), may hold values from -0.125 to 0.125
- block_ids: int32 [16, 40, 16], P('col', 'tok'), may hold values from 0 to 39, as said below
- block_counts: int32 [16, 40], P('col', 'tok'), may hold values from 1 to 16, as said below
Outputs:
- mixed: bfloat16 [2560, 4096], P('tok', 'col')
Inputs may be any that keep to these rules, and one draw needn't show every extreme that they name: block_ids[h, b, 0] = b; the slots below block_counts[h, b] hold distinct blocks none after b; later slots hold block numbers that are not read. block_counts[h, b] <= b + 1; densities differ from head to head, and some row of some head uses all 16 slots.
All inputs are finite; a program needn't handle non-finite values.
Results may differ from a plain program's by a relative error of at most 0.012.
Values may be sent and summed in bfloat16 or wider, within the bound.
No kernel may reach another device: no remote copies, remote signals or barrier semaphores. Data moves between devices by JAX's collectives and lax.ppermute only.
A program may use at most 64 MiB of HBM per device.

v0:
```python
import jax
import jax.numpy as jnp
from jax import lax
from jax.sharding import PartitionSpec as P

HEAD_SIZE = 128
BLK = 64
NSEL = 16
rope_base = 500000.0


def rotate(field, positions):
    half = field.shape[-1] // 2
    freq = rope_base ** (-jnp.arange(half, dtype=jnp.float32) / half)
    angle = positions[:, None] * freq[None, :]
    cosine = jnp.cos(angle)[:, None, :]
    sine = jnp.sin(angle)[:, None, :]
    first = field[..., :half]
    second = field[..., half:]
    return jnp.concatenate(
        [first * cosine - second * sine, second * cosine + first * sine], axis=-1
    )


def on_device(tokens, w_query, w_key, w_value, w_out, block_ids, block_counts):
    tok_rows = tokens.shape[0]
    head_local = w_query.shape[1] // HEAD_SIZE
    kv_local = w_key.shape[1] // HEAD_SIZE
    group_size = head_local // kv_local
    blocks_dev = block_ids.shape[1]
    piece = lax.all_gather(tokens, "col", axis=1, tiled=True)
    width = piece.shape[1]

    def product(weight):
        return jnp.dot(piece, weight, preferred_element_type=jnp.float32)

    query_raw = product(w_query)
    key_raw = product(w_key)
    value_raw = product(w_value)
    tok_place = lax.axis_index("tok")
    query_index = tok_place * tok_rows + jnp.arange(tok_rows, dtype=jnp.int32)
    positions = query_index.astype(jnp.float32)
    query_rows = rotate(query_raw.reshape(tok_rows, head_local, HEAD_SIZE), positions).astype(
        jnp.bfloat16
    )
    keys = rotate(key_raw.reshape(tok_rows, kv_local, HEAD_SIZE), positions).astype(jnp.bfloat16)
    values = value_raw.astype(jnp.bfloat16).reshape(tok_rows, kv_local, HEAD_SIZE)
    grouped = query_rows.reshape(tok_rows, kv_local, group_size, HEAD_SIZE)
    live = jnp.arange(NSEL, dtype=jnp.int32)[None, None, :] < block_counts[:, :, None]
    last_query = tok_place * tok_rows + tok_rows - 1
    start_state = (
        jnp.full((head_local, tok_rows), -1e30, jnp.float32),
        jnp.zeros((head_local, tok_rows), jnp.float32),
        jnp.zeros((head_local, tok_rows, HEAD_SIZE), jnp.float32),
    )
    key_part = lax.all_gather(keys, "tok", axis=0, tiled=True)
    value_part = lax.all_gather(values, "tok", axis=0, tiled=True)
    amount = key_part.shape[0]
    width = 512
    key_blocks = key_part.reshape(amount // width, width, kv_local, HEAD_SIZE)
    value_blocks = value_part.reshape(amount // width, width, kv_local, HEAD_SIZE)
    offsets = jnp.arange(amount // width, dtype=jnp.int32) * width

    def one_block(state, inputs):
        key_block, value_block, offset = inputs

        def compute(inner_state):
            highest, total, summed_weights = inner_state
            key_index = offset + jnp.arange(width, dtype=jnp.int32)
            key_group = key_index // BLK
            hit = jnp.any(
                (block_ids[:, :, :, None] == key_group[None, None, None, :]) & live[..., None],
                axis=2,
            )
            allowed = jnp.broadcast_to(hit[:, :, None, :], (head_local, blocks_dev, BLK, width))
            allowed = allowed.reshape(head_local, tok_rows, width)
            allowed = allowed & (key_index[None, None, :] <= query_index[None, :, None])
            logit_scores = jnp.einsum(
                "tcgd,kcd->cgtk", grouped, key_block, preferred_element_type=jnp.float32
            )
            logit_scores = logit_scores.reshape(head_local, tok_rows, width) * HEAD_SIZE ** (-0.5)
            masked = jnp.where(allowed, logit_scores, -1e30)
            fresh = jnp.maximum(highest, jnp.max(masked, axis=-1))
            decay = jnp.exp(highest - fresh)
            weights = jnp.where(allowed, jnp.exp(masked - fresh[..., None]), 0.0)
            total = total * decay + jnp.sum(weights, axis=-1)
            rounded_scores = weights.astype(jnp.bfloat16).reshape(
                kv_local, group_size, tok_rows, width
            )
            added = jnp.einsum(
                "cgtk,kcd->cgtd", rounded_scores, value_block, preferred_element_type=jnp.float32
            )
            summed_weights = summed_weights * decay[..., None] + added.reshape(
                head_local, tok_rows, HEAD_SIZE
            )
            return (fresh, total, summed_weights)

        return (
            lax.cond(offset > last_query, lambda inner_state: inner_state, compute, state),
            None,
        )

    result, _ = lax.scan(one_block, start_state, (key_blocks, value_blocks, offsets))
    highest, total, summed_weights = result
    attended = jnp.transpose((summed_weights / total[..., None]).astype(jnp.bfloat16), (1, 0, 2))
    flat = attended.reshape(tok_rows, head_local * HEAD_SIZE)
    summed_out = lax.psum_scatter(
        lax.dot_general(
            w_out, flat, (((0,), (1,)), ((), ())), preferred_element_type=jnp.float32
        ).astype(jnp.bfloat16),
        "col",
        scatter_dimension=0,
        tiled=True,
    ).astype(jnp.float32)
    return jnp.transpose(summed_out).astype(jnp.bfloat16)


def solution(mesh):
    in_specs = (
        P("tok", "col"),
        P(None, "col"),
        P(None, "col"),
        P(None, "col"),
        P("col", None),
        P("col", "tok", None),
        P("col", "tok"),
    )
    out_specs = P("tok", "col")
    return jax.shard_map(
        on_device, mesh=mesh, in_specs=in_specs, out_specs=out_specs, check_vma=False
    )
```

profile of v0, /device:TPU:0, one launch (start us, length us, event | category | flops | bytes accessed | tf_op | source)
XLA Modules:
  0.0 185.4 jit_solution(4791514653528160586)
XLA Ops:
  6.5 0.7 all-gather.3.cloned.1.call-update
  7.3 0.7 copy.25
  8.0 0.6 multiply_cosine_fusion
  8.7 28.5 %all-gather.3.cloned.1.call-done = bf16[320,4096]{1,0:T(8,128)(2,1)} async-done(((bf16[320,1024]{1,0:T(8,128)(2,1)}), bf16[320,4096]{1,0:T(8,128)(2,1)}) %all-gather.3.cloned.1.call-update) | async-done | bytes 2621456 | tf_op jit(solution)/shard_map/all_gather | solution.py:31
  37.2 4.5 %fusion.43 = f32[320,512]{1,0:T(8,128)S(1)} fusion(bf16[320,4096]{1,0:T(8,128)(2,1)} %all-gather.3.cloned.1.call-done, bf16[4096,512]{1,0:T(8,128)(2,1)} %param.12), kind=kOutput, calls=%fused_computation.67 | convolution fusion | flops 1342177280 | bytes 7471104 | tf_op jit(solution)/shard_map/dot_general | solution.py:35
  42.3 1.3 copy-done.1
  43.7 0.8 convolution_bitcast_fusion
  44.5 0.7 fusion.39
  45.3 31.9 %all_gather.10 = bf16[2560,1,128]{2,0,1:T(8,128)(2,1)S(1)} all-gather(bf16[320,1,128]{2,0,1:T(8,128)(2,1)S(1)} %pad_maximum_fusion.1), channel_id=1, replica_groups=mesh['tok'=8,'col'=4] {'tok'}, dimensions={0}, use_global_device_ids=true | all-gather | bytes 737280 | tf_op jit(solution)/shard_map/all_gather | solution.py:56
  77.3 0.8 convolution_convert_fusion.1
  78.2 31.4 %all-gather = bf16[2560,128]{1,0:T(8,128)(2,1)S(1)} all-gather(bf16[320,128]{1,0:T(8,128)(2,1)S(1)} %convolution_convert_fusion.1), channel_id=2, replica_groups=mesh['tok'=8,'col'=4] {'tok'}, dimensions={0}, use_global_device_ids=true | all-gather | bytes 737280 | tf_op jit(solution)/shard_map/all_gather | solution.py:57
  110.0 11.1 %while.15 = (s32[]{:T(128)}, f32[4,320]{1,0:T(4,128)S(1)}, f32[4,320]{1,0:T(4,128)S(1)}, f32[4,320,128]{2,1,0:T(8,128)S(1)}, s32[5]{0:T(128)S(1)}, /*index=5*/s3...) while((s32[]{:T(128)}, f32[4,320]{1,0:T(4,128)S(1)}, ...), condition=%wide.region_6.7_spmd.clone, body=%wide.region_0.6_spmd.clone.sunk | while | flops 347014272 | bytes 13164303 | solution.py:103
  110.0 0.6 dynamic_slice.33
  111.3 4.4 %conditional.3 = (f32[4,320]{1,0:T(4,128)S(1)}, f32[4,320]{1,0:T(4,128)S(1)}, f32[4,320,128]{2,1,0:T(8,128)S(1)}) conditional(s32[]{:T(128)} %convert_element_type.74, (s32[4,5,16]{2,1,0:T(8,128)S(1)}, s32[]{:T(128)}, s32[4,5,16]{2,1,0:T(8,128)S(1)}, s32[]{:T(128)}, bf16[5,512,1,128]{3,1,2,0:T(8,128)(2,1)S(1)}, /*index=5*/s32[]{:T(128)}, ...), branch_computations={%region_1.4_spmd, %region_5.5_spmd} | conditional | flops 347014272 | bytes 13151224 | solution.py:99
  111.3 0.6 add_select_fusion
  112.7 0.8 fusion.4
  113.5 1.1 fusion.6
  114.6 1.0 fusion.11
  115.7 0.6 dynamic_slice.33
  117.0 0.6 dynamic_slice.33
  118.4 0.6 dynamic_slice.33
  119.7 0.6 dynamic_slice.33
  121.1 5.3 %fusion.28 = bf16[4096,320]{0,1:T(8,128)(2,1)} fusion(bf16[512,4096]{1,0:T(8,128)(2,1)} %param.15, f32[4,320,128]{2,1,0:T(8,128)S(1)} %get-tuple-element.165, f32[4,320]{1,0:T(4,128)S(1)} %get-tuple-element.166), kind=kOutput, calls=%fused_computation.38 | convolution fusion | flops 1343815680 | bytes 7476224 | tf_op jit(solution)/shard_map/dot_general | solution.py:108
  126.4 52.1 %reduce-scatter.2.cloned.1.call-done = bf16[1024,320]{0,1:T(8,128)(2,1)} async-done(((bf16[4096,320]{0,1:T(8,128)(2,1)}), bf16[1024,320]{0,1:T(8,128)(2,1)}) %reduce-scatter.2.cloned.1.call-update) | async-done | bytes 655376 | tf_op jit(solution)/shard_map/reduce_scatter | solution.py:107
  (51 shorter events, 2.1 us)
Async XLA Ops:
  6.5 35.8 %copy-start = (bf16[4096,128]{1,0:T(8,128)(2,1)S(1)}, bf16[4096,128]{1,0:T(8,128)(2,1)}, u32[]{:S(2)}) copy-start(bf16[4096,128]{1,0:T(8,128)(2,1)} %param.13) | copy-start | bytes 3145732
  6.5 30.6 %all-gather.3.cloned.1.call-start = ((), (), s32[]{:S(2)}) async-start(), calls=%async_computation.1 | async-start | bytes 3276800 | tf_op jit(solution)/shard_map/all_gather | solution.py:31
  7.3 171.3 %reduce-scatter.2.cloned.1.call-start = ((), (), s32[]{:S(2)}) async-start(), calls=%async_computation.2 | async-start | bytes 3276800 | tf_op jit(solution)/shard_map/reduce_scatter | solution.py:107
  41.9 1.7 copy-start.1
  43.7 33.6 %copy-start.2 = (bf16[4096,128]{1,0:T(8,128)(2,1)S(1)}, bf16[4096,128]{1,0:T(8,128)(2,1)}, u32[]{:S(2)}) copy-start(bf16[4096,128]{1,0:T(8,128)(2,1)} %param.14) | copy-start | bytes 3145732
  78.1 31.9 %copy-start.3 = (s32[4,5]{1,0:T(4,128)S(1)}, s32[4,5]{1,0:T(4,128)}, u32[]{:S(2)}) copy-start(s32[4,5]{1,0:T(4,128)} %param.17) | copy-start | bytes 244
Sparse Core Ops, SparseCore 0:
  8.9 28.2 all-gather.2
  126.5 51.9 reduce-scatter.1
where the time goes:
time: 186 us; the launch traced here: 185 us
  waiting for transfers between devices  81.4 us (44%)
  blocking collectives  63.3 us (34%)
  between operations  13.5 us (7%)
  matrix products  13.4 us (7%)
  local copies, waits for them, and re-layouts  6.13 us (3%)
  other arithmetic  4.08 us (2%)
  loops' own time  3.5 us (2%)
    reduce_scatter x1, waiting for transfers between devices, on_device(): lax.psum_scatter(lax.dot_general(w_out, flat, (((0,), (1,)), ((), ())), p...  52.1 us
    all_gather x1, blocking collectives, on_device(): key_part = lax.all_gather(keys, 'tok', axis=0, tiled=True)  31.9 us
    all_gather x1, blocking collectives, on_device(): value_part = lax.all_gather(values, 'tok', axis=0, tiled=True)  31.4 us
    all_gather x1, waiting for transfers between devices, on_device(): piece = lax.all_gather(tokens, 'col', axis=1, tiled=True)  28.5 us
    dot_general x3, matrix products, product(): return jnp.dot(piece, weight, preferred_element_type=jnp.float32)  6.19 us
    dot_general x1, matrix products, on_device(): lax.dot_general(w_out, flat, (((0,), (1,)), ((), ())), preferred_element_...  5.31 us
  transfers between devices with their start and end apart: 2, of which 2 were waited for; matrix products, arithmetic and copies ran while one was open for 1% of the time, Pallas kernels for 0%

commit v1 on v0

--- a/solution.py
+++ b/solution.py
@@ -7,6 +7,28 @@
 BLK = 64
 NSEL = 16
 rope_base = 500000.0
+
+
+def joined_along(tiles, dim):
+    dims = list(tiles.shape[1:])
+    dims[dim] *= tiles.shape[0]
+    return jnp.moveaxis(tiles, 0, dim).reshape(dims)
+
+
+def collected_by_bits(x, axis):
+    size = lax.axis_size(axis)
+    blocks = x[None]
+    for level in range(size.bit_length() - 1):
+        apart = 1 << level
+        received = lax.ppermute(blocks, axis, [(i, i ^ apart) for i in range(size)])
+        both = jnp.stack([blocks, received])
+        upper = lax.axis_index(axis) >> level & 1
+        blocks = jnp.where(upper == 0, both, both[::-1]).reshape(-1, *x.shape)
+    return blocks
+
+
+def doubled_up(x, axis, dim):
+    return joined_along(collected_by_bits(x, axis), dim)
 
 
 def rotate(field, positions):
@@ -53,7 +75,7 @@
         jnp.zeros((head_local, tok_rows), jnp.float32),
         jnp.zeros((head_local, tok_rows, HEAD_SIZE), jnp.float32),
     )
-    key_part = lax.all_gather(keys, "tok", axis=0, tiled=True)
+    key_part = doubled_up(keys, "tok", 0)
     value_part = lax.all_gather(values, "tok", axis=0, tiled=True)
     amount = key_part.shape[0]
     width = 512

time: 186 us -> 170 us (0.914)
  blocking collectives: 63.3 us -> 37 us
  starting transfers between devices: 0.04 us -> 5.59 us
  matrix products: 13.4 us -> 17.1 us
    all_gather x1 -> x0, blocking collectives: 31.9 us -> none  [on_device(): key_part = lax.all_gather(keys, 'tok', axis=0, tiled=True)]
    all_gather x1, blocking collectives: 31.4 us -> 37 us  [on_device(): value_part = lax.all_gather(values, 'tok', axis=0, tiled=True)]
    ppermute x0 -> x3, starting transfers between devices: none -> 5.55 us  [collected_by_bits(): received = lax.ppermute(blocks, axis, [(i, i ^ apart) for i in range(size)])]
    ppermute x0 -> x3, waiting for transfers between devices: none -> 4.4 us  [collected_by_bits(): received = lax.ppermute(blocks, axis, [(i, i ^ apart) for i in range(size)])]
    dot_general x3, matrix products: 6.19 us -> 9.89 us  [product(): return jnp.dot(piece, weight, preferred_element_type=jnp.float32)]
    reduce_scatter x1, waiting for transfers between devices: 52.1 us -> 49 us  [on_device(): lax.psum_scatter(lax.dot_general(w_out, flat, (((0,), (1,)), ((), ())), p...]
  transfers between devices with their start and end apart: 2 -> 5, of which waited for: 2 -> 3; matrix products, arithmetic and copies ran while one was open for 1% -> 6% of each run, Pallas kernels for 0% -> 0%
where the time goes in v1:
time: 170 us
  waiting for transfers between devices  82.6 us (49%)
  blocking collectives  37 us (22%)
  matrix products  17.1 us (10%)
  between operations  13.6 us (8%)
  local copies, waits for them, and re-layouts  5.64 us (3%)
  starting transfers between devices  5.59 us (3%)
  other arithmetic  4.54 us (3%)
  loops' own time  3.61 us (2%)
    reduce_scatter x1, waiting for transfers between devices, on_device(): lax.psum_scatter(lax.dot_general(w_out, flat, (((0,), (1,)), ((), ())), p...  49 us
    all_gather x1, blocking collectives, on_device(): value_part = lax.all_gather(values, 'tok', axis=0, tiled=True)  37 us
    all_gather x1, waiting for transfers between devices, on_device(): piece = lax.all_gather(tokens, 'col', axis=1, tiled=True)  28.5 us
    dot_general x3, matrix products, product(): return jnp.dot(piece, weight, preferred_element_type=jnp.float32)  9.89 us
    ppermute x3, starting transfers between devices, collected_by_bits(): received = lax.ppermute(blocks, axis, [(i, i ^ apart) for i in range(size)])  5.55 us
    dot_general x1, matrix products, on_device(): lax.dot_general(w_out, flat, (((0,), (1,)), ((), ())), preferred_element_...  5.31 us
    ppermute x3, waiting for transfers between devices, collected_by_bits(): received = lax.ppermute(blocks, axis, [(i, i ^ apart) for i in range(size)])  4.4 us
    another operation x1, loops' own time, on_device(): lax.scan(one_block, start_state, (key_blocks, value_blocks, offsets))  3.44 us
  transfers between devices with their start and end apart: 5, of which 3 were waited for; matrix products, arithmetic and copies ran while one was open for 6% of the time, Pallas kernels for 0%

profile of v1, /device:TPU:0, one launch (start us, length us, event | category | flops | bytes accessed | tf_op | source)
XLA Modules:
  0.0 169.6 jit_solution(1893614936240478748)
XLA Ops:
  6.5 0.7 all-gather.3.cloned.1.call-update
  7.3 0.7 copy.23
  8.1 0.6 multiply_cosine_fusion
  8.7 28.5 %all-gather.3.cloned.1.call-done = bf16[320,4096]{1,0:T(8,128)(2,1)} async-done(((bf16[320,1024]{1,0:T(8,128)(2,1)}), bf16[320,4096]{1,0:T(8,128)(2,1)}) %all-gather.3.cloned.1.call-update) | async-done | bytes 2621456 | tf_op jit(solution)/shard_map/all_gather | solution.py:53
  37.2 2.7 %convolution_bitcast_fusion = f32[320,1,128]{2,0,1:T(8,128)S(1)} fusion(bf16[320,4096]{1,0:T(8,128)(2,1)} %all-gather.3.cloned.1.call-done, bf16[4096,128]{1,0:T(8,128)(2,1)S(1)} %copy-done), kind=kOutput, calls=%fused_computation.39 | convolution fusion | flops 335544320 | bytes 3833856 | tf_op jit(solution)/shard_map/dot_general | solution.py:57
  39.9 0.7 fusion.39
  40.8 1.5 collective-permute-start
  42.3 4.6 %fusion.45 = f32[320,512]{1,0:T(8,128)} fusion(bf16[320,4096]{1,0:T(8,128)(2,1)S(1)} %copy-done.1, bf16[4096,512]{1,0:T(8,128)(2,1)} %param.12), kind=kOutput, calls=%fused_computation.75 | convolution fusion | flops 1342177280 | bytes 7471104 | tf_op jit(solution)/shard_map/dot_general | solution.py:57
  46.9 1.3 reshape.385
  48.2 2.6 %convolution_convert_fusion.1 = bf16[320,128]{1,0:T(8,128)(2,1)S(1)} fusion(bf16[320,4096]{1,0:T(8,128)(2,1)} %all-gather.3.cloned.1.call-done, bf16[4096,128]{1,0:T(8,128)(2,1)S(1)} %copy-done.2), kind=kOutput, calls=%fused_computation.40 | convolution fusion | flops 335585280 | bytes 3751936 | tf_op jit(solution)/shard_map/dot_general | solution.py:57
  51.3 1.6 collective-permute-start.1
  53.1 4.4 %collective-permute-done.1 = bf16[2,320,1,128]{3,1,0,2:T(8,128)(2,1)S(1)} collective-permute-done((bf16[2,320,1,128]{3,1,0,2:T(8,128)(2,1)S(1)}, bf16[2,320,1,128]{3,1,0,2:T(8,128)(2,1)S(1)}, u32[]{:S(2)}, u32[]{:S(2)}) %collective-permute-start.1) | collective-permute-done | bytes 163872 | tf_op jit(solution)/shard_map/ppermute | solution.py:23
  57.6 2.5 %collective-permute-start.2 = (bf16[4,320,1,128]{3,1,0,2:T(8,128)(2,1)S(1)}, bf16[4,320,1,128]{3,1,0,2:T(8,128)(2,1)S(1)}, u32[]{:S(2)}, u32[]{:S(2)}) collective-permute-start(bf16[4,320,1,128]{3,1,0,2:T(8,128)(2,1)S(1)} %bitcast.88), channel_id=1, source_target_pairs={{0,16},{4,20},{8,24},{12,28},{16,0},{20,4},{24,8},{28,12},{1,17},{... | collective-permute-start | bytes 983048 | tf_op jit(solution)/shard_map/ppermute | solution.py:23
  60.2 37.0 %all-gather = bf16[2560,128]{1,0:T(8,128)(2,1)S(1)} all-gather(bf16[320,128]{1,0:T(8,128)(2,1)S(1)} %convolution_convert_fusion.1), channel_id=2, replica_groups=mesh['tok'=8,'col'=4] {'tok'}, dimensions={0}, use_global_device_ids=true | all-gather | bytes 737280 | tf_op jit(solution)/shard_map/all_gather | solution.py:79
  97.6 10.9 %while.15 = (s32[]{:T(128)}, f32[4,320]{1,0:T(4,128)S(1)}, f32[4,320]{1,0:T(4,128)S(1)}, f32[4,320,128]{2,1,0:T(8,128)S(1)}, s32[5]{0:T(128)S(1)}, /*index=5*/s3...) while((s32[]{:T(128)}, f32[4,320]{1,0:T(4,128)S(1)}, ...), condition=%wide.region_6.7_spmd.clone, body=%wide.region_0.6_spmd.clone.sunk | while | flops 347014272 | bytes 13164303 | solution.py:125
  97.6 0.6 dynamic_slice.33
  98.8 4.4 %conditional.3 = (f32[4,320]{1,0:T(4,128)S(1)}, f32[4,320]{1,0:T(4,128)S(1)}, f32[4,320,128]{2,1,0:T(8,128)S(1)}) conditional(s32[]{:T(128)} %convert_element_type.82, (s32[4,5,16]{2,1,0:T(8,128)S(1)}, s32[]{:T(128)}, s32[4,5,16]{2,1,0:T(8,128)S(1)}, s32[]{:T(128)}, bf16[5,512,1,128]{3,1,2,0:T(8,128)(2,1)S(1)}, /*index=5*/s32[]{:T(128)}, ...), branch_computations={%region_1.4_spmd, %region_5.5_spmd} | conditional | flops 347014272 | bytes 13151224 | solution.py:121
  98.8 0.7 add_select_fusion
  100.2 0.8 fusion.4
  101.0 1.1 fusion.6
  102.2 1.0 fusion.11
  103.3 0.6 dynamic_slice.33
  108.5 5.3 %fusion.28 = bf16[4096,320]{0,1:T(8,128)(2,1)} fusion(bf16[512,4096]{1,0:T(8,128)(2,1)} %param.15, f32[4,320,128]{2,1,0:T(8,128)S(1)} %get-tuple-element.165, f32[4,320]{1,0:T(4,128)S(1)} %get-tuple-element.166), kind=kOutput, calls=%fused_computation.38 | convolution fusion | flops 1343815680 | bytes 7476224 | tf_op jit(solution)/shard_map/dot_general | solution.py:130
  113.8 49.0 %reduce-scatter.2.cloned.1.call-done = bf16[1024,320]{0,1:T(8,128)(2,1)} async-done(((bf16[4096,320]{0,1:T(8,128)(2,1)}), bf16[1024,320]{0,1:T(8,128)(2,1)}) %reduce-scatter.2.cloned.1.call-update) | async-done | bytes 655376 | tf_op jit(solution)/shard_map/reduce_scatter | solution.py:129
  (62 shorter events, 4.1 us)
Async XLA Ops:
  6.5 30.7 %copy-start = (bf16[4096,128]{1,0:T(8,128)(2,1)S(1)}, bf16[4096,128]{1,0:T(8,128)(2,1)}, u32[]{:S(2)}) copy-start(bf16[4096,128]{1,0:T(8,128)(2,1)} %param.13) | copy-start | bytes 3145732
  6.5 30.6 %all-gather.3.cloned.1.call-start = ((), (), s32[]{:S(2)}) async-start(), calls=%async_computation.1 | async-start | bytes 3276800 | tf_op jit(solution)/shard_map/all_gather | solution.py:53
  7.3 155.5 %reduce-scatter.2.cloned.1.call-start = ((), (), s32[]{:S(2)}) async-start(), calls=%async_computation.2 | async-start | bytes 3276800 | tf_op jit(solution)/shard_map/reduce_scatter | solution.py:129
  37.2 5.1 %copy-start.1 = (bf16[320,4096]{1,0:T(8,128)(2,1)S(1)}, bf16[320,4096]{1,0:T(8,128)(2,1)}, u32[]{:S(2)}) copy-start(bf16[320,4096]{1,0:T(8,128)(2,1)} %all-gather.3.cloned.1.call-done) | copy-start | bytes 7864324
  40.7 7.4 %copy-start.2 = (bf16[4096,128]{1,0:T(8,128)(2,1)S(1)}, bf16[4096,128]{1,0:T(8,128)(2,1)}, u32[]{:S(2)}) copy-start(bf16[4096,128]{1,0:T(8,128)(2,1)} %param.14) | copy-start | bytes 3145732
  40.8 10.4 %collective-permute-start = (bf16[1,320,1,128]{3,1,2,0:T(8,128)(2,1)S(1)}, bf16[1,320,1,128]{3,1,2,0:T(8,128)(2,1)S(1)}, u32[]{:S(2)}, u32[]{:S(2)}) collective-permute-start(bf16[1,320,1,128]{3,1,2,0:T(8,128)(2,1)S(1)} %pad_maximum_fusion.4), channel_id=1, source_target_pairs={{0,4},{4,0},{8,12},{12,8},{16,20},{20,16},{24,28},{28,24},{1,5},{5... | collective-permute-start | bytes 245768 | tf_op jit(solution)/shard_map/ppermute | solution.py:23
  51.3 6.1 %collective-permute-start.1 = (bf16[2,320,1,128]{3,1,0,2:T(8,128)(2,1)S(1)}, bf16[2,320,1,128]{3,1,0,2:T(8,128)(2,1)S(1)}, u32[]{:S(2)}, u32[]{:S(2)}) collective-permute-start(bf16[2,320,1,128]{3,1,0,2:T(8,128)(2,1)S(1)} %get-tuple-element.278), channel_id=1, source_target_pairs={{0,8},{4,12},{8,0},{12,4},{16,24},{20,28},{24,16},{28,20},{1,9},{5... | collective-permute-start | bytes 491528 | tf_op jit(solution)/shard_map/ppermute | solution.py:23
  57.6 40.0 %copy-start.3 = (s32[4,5]{1,0:T(4,128)S(1)}, s32[4,5]{1,0:T(4,128)}, u32[]{:S(2)}) copy-start(s32[4,5]{1,0:T(4,128)} %param.17) | copy-start | bytes 244
  57.6 39.7 %collective-permute-start.2 = (bf16[4,320,1,128]{3,1,0,2:T(8,128)(2,1)S(1)}, bf16[4,320,1,128]{3,1,0,2:T(8,128)(2,1)S(1)}, u32[]{:S(2)}, u32[]{:S(2)}) collective-permute-start(bf16[4,320,1,128]{3,1,0,2:T(8,128)(2,1)S(1)} %bitcast.88), channel_id=1, source_target_pairs={{0,16},{4,20},{8,24},{12,28},{16,0},{20,4},{24,8},{28,12},{1,17},{... | collective-permute-start | bytes 983048 | tf_op jit(solution)/shard_map/ppermute | solution.py:23
Sparse Core Ops, SparseCore 0:
  8.9 28.2 all-gather.2
  113.9 48.7 reduce-scatter.1
